TPU v7x, 32 devices: a whole 2x2x4 slice. The times are simulated.
32 devices in a mesh: groups: 2 (over y), node: 4 (over z), rep: 4 (over x, core).
Axes of the slice: x: 2, y: 2, z: 4, core: 2. Of those that a mesh axis runs over, the one named last changes fastest.
Arguments:
- node_states: bfloat16 [8, 512, 512], P(('groups', 'rep'), 'node'), parts along dimension 0, may hold values from -6 to 6
- cotangent: bfloat16 [8, 512, 512], P(('groups', 'rep'), 'node'), parts along dimension 0, may hold values from -1.1953125 to 1.1953125
- reach_blocks: int32 [8, 8, 8], P(('groups', 'rep'), 'node'), parts along dimension 0, may hold values from 0 to 7, as said below
- reach_count: int32 [8, 8], P(('groups', 'rep'), 'node'), parts along dimension 0, may hold values from 1 to 8, as said below
- level_start: int32 [8, 17], P(('groups', 'rep')), parts along dimension 0, may hold values from 0 to 512, as said below
- query_weight: bfloat16 [512, 256], replicated, may hold values from -0.25 to 0.25
- key_weight: bfloat16 [512, 256], replicated, may hold values from -0.25 to 0.25
- value_weight: bfloat16 [512, 256], replicated, may hold values from -0.25 to 0.25
- out_weight: bfloat16 [256, 512], replicated, may hold values from -0.375 to 0.375
- bias_table: float32 [4, 32], replicated, may hold values from -4 to 412
Outputs:
- updated: bfloat16 [8, 512, 512], P(('groups', 'rep'), 'node'), parts along dimension 0
- node_state_gradient: bfloat16 [8, 512, 512], P(('groups', 'rep'), 'node'), parts along dimension 0
- grad_query: float32 [1024, 256], P('groups'), parts along dimension 0
- grad_key: float32 [1024, 256], P('groups'), parts along dimension 0
- grad_value: float32 [1024, 256], P('groups'), parts along dimension 0
- grad_out: float32 [512, 512], P('groups'), parts along dimension 0
There are 2 independent parts, one for each index of `groups`. A program takes and returns all parts, laid end to end along the dimension named above; an argument that names none is the same for every part. Nothing has to cross between parts.
Inputs may be any that keep to these rules, and one draw needn't show every extreme that they name: `reach_blocks`: in row b of a graph, entry 0 is b, entries 1 to min(b, 7) are distinct blocks below b, and any later entries are b. `reach_count`: row b holds at most b + 1; row 7 of every graph holds 8. `level_start`: strictly increasing; entry 0 is 0 and entry 16 is 512.
All inputs are finite; a program needn't handle non-finite values.
Results may differ from a plain program's by a relative error of at most 0.011.
Values may be sent and summed in bfloat16 or wider, within the bound.
No kernel may reach another device: no remote copies, remote signals or barrier semaphores. Data moves between devices by JAX's collectives and lax.ppermute only.
A program may use at most 64 MiB of HBM per device.

v0:
```python
import jax
import jax.numpy as jnp
from jax import lax
from jax.sharding import PartitionSpec as P

HEADS = 4
HEAD = 64
BLOCK = 64
DIST = 32
EPS = 1e-05
NEG = -1e30
HIGH = lax.Precision.HIGHEST
CONTRACT_ROWS = (((0,), (0,)), ((), ()))
CONTRACT_COLS = (((1,), (1,)), ((), ()))


def rows_product(left, right):
    return lax.dot_general(left, right, CONTRACT_ROWS, preferred_element_type=jnp.float32)


def cols_product(left, right):
    return lax.dot_general(left, right, CONTRACT_COLS, preferred_element_type=jnp.float32)


def expand(listed):
    return jnp.repeat(jnp.repeat(listed, BLOCK, axis=0), BLOCK, axis=1)


def level_tables(starts, total, bias_table):
    level_count = starts.shape[0] - 1
    places = jnp.arange(total, dtype=jnp.int32)
    inner = starts[1:level_count]
    levels = jnp.sum((places[:, None] >= inner[None, :]).astype(jnp.int32), axis=1)
    marks = jnp.arange(level_count, dtype=jnp.int32)
    onehot = (levels[:, None] == marks[None, :]).astype(jnp.float32)
    spread = jnp.clip(marks[:, None] - marks[None, :], 0, DIST - 1)
    picks = (spread[:, :, None] == jnp.arange(DIST, dtype=jnp.int32)[None, None, :]).astype(
        jnp.float32
    )
    level_bias = jnp.einsum("hd,abd->hab", bias_table, picks, precision=HIGH)
    return (levels, onehot, level_bias)


def bias_block(row_onehot, head_bias, col_onehot):
    row_part = jnp.dot(row_onehot, head_bias, precision=HIGH)
    return lax.dot_general(row_part, col_onehot, CONTRACT_COLS, precision=HIGH)


def on_device(
    node_states,
    cotangent,
    reach_blocks,
    reach_count,
    level_start,
    query_weight,
    key_weight,
    value_weight,
    out_weight,
    bias_table,
):
    states = node_states[0]
    grads_in = cotangent[0]
    blocks = reach_blocks[0]
    counts = reach_count[0]
    starts = level_start[0]
    rows_dev = states.shape[0]
    width = query_weight.shape[1]
    total = rows_dev * lax.axis_size("node")
    offset = lax.axis_index("node") * rows_dev
    scale = HEAD ** (-0.5)
    key_blocks = total // BLOCK
    states_single_float = states.astype(jnp.float32)
    inverse_norm_scale = lax.rsqrt(
        jnp.mean(states_single_float * states_single_float, axis=1, keepdims=True) + EPS
    )
    centered_states = states_single_float * inverse_norm_scale
    normalized_states = centered_states.astype(jnp.bfloat16)
    queries = jnp.dot(normalized_states, query_weight, preferred_element_type=jnp.float32).astype(
        jnp.bfloat16
    )
    keys = jnp.dot(normalized_states, key_weight, preferred_element_type=jnp.float32).astype(
        jnp.bfloat16
    )
    values = jnp.dot(normalized_states, value_weight, preferred_element_type=jnp.float32).astype(
        jnp.bfloat16
    )
    keys_all, values_all = (
        lax.all_gather(keys, "node", axis=0, tiled=True),
        lax.all_gather(values, "node", axis=0, tiled=True),
    )
    levels, onehot, level_bias = level_tables(starts, total, bias_table)
    positions = jnp.arange(total, dtype=jnp.int32)
    local = jnp.arange(rows_dev, dtype=jnp.int32)
    row_ids = offset + local
    row_levels = lax.dynamic_slice_in_dim(levels, offset, rows_dev, 0)
    row_onehot = lax.dynamic_slice_in_dim(onehot, offset, rows_dev, 0)
    slots = jnp.arange(blocks.shape[1], dtype=jnp.int32)
    live = slots[None, :] < counts[:, None]
    kinds = jnp.arange(key_blocks, dtype=jnp.int32)
    listed = jnp.any((blocks[:, :, None] == kinds[None, None, :]) & live[:, :, None], axis=1)
    visible = expand(listed) & (
        (levels[None, :] < row_levels[:, None]) | (positions[None, :] == row_ids[:, None])
    )
    prob_list = []
    lse_list = []
    mixed_list = []
    for head in range(HEADS):
        lower = head * HEAD
        scores = (
            cols_product(queries[:, lower : lower + HEAD], keys_all[:, lower : lower + HEAD])
            * scale
        )
        scores = scores + bias_block(row_onehot, level_bias[head], onehot)
        scores = jnp.where(visible, scores, NEG)
        peak = jnp.max(scores, axis=1, keepdims=True)
        mass = jnp.sum(jnp.where(visible, jnp.exp(scores - peak), 0.0), axis=1, keepdims=True)
        lse = peak + jnp.log(mass)
        probs = jnp.where(visible, jnp.exp(scores - lse), 0.0).astype(jnp.bfloat16)
        prob_list.append(probs)
        lse_list.append(lse)
        mixed_list.append(
            jnp.dot(probs, values_all[:, lower : lower + HEAD], preferred_element_type=jnp.float32)
        )
    mixed = jnp.concatenate(mixed_list, axis=1).astype(jnp.bfloat16)
    updated = (
        states_single_float + jnp.dot(mixed, out_weight, preferred_element_type=jnp.float32)
    ).astype(jnp.bfloat16)
    partial_out = rows_product(mixed, grads_in)
    d_mixed = cols_product(grads_in, out_weight).astype(jnp.bfloat16)
    score_grads = []
    delta_list = []
    query_grads = []
    for head in range(HEADS):
        lower = head * HEAD
        mixed_head = d_mixed[:, lower : lower + HEAD]
        delta = jnp.sum(
            mixed_head.astype(jnp.float32) * mixed[:, lower : lower + HEAD].astype(jnp.float32),
            axis=1,
            keepdims=True,
        )
        d_probs = cols_product(mixed_head, values_all[:, lower : lower + HEAD])
        d_scores = (prob_list[head].astype(jnp.float32) * (d_probs - delta)).astype(jnp.bfloat16)
        score_grads.append(d_scores)
        delta_list.append(delta)
        query_grads.append(
            jnp.dot(d_scores, keys_all[:, lower : lower + HEAD], preferred_element_type=jnp.float32)
            * scale
        )
    d_queries = jnp.concatenate(query_grads, axis=1).astype(jnp.bfloat16)
    key_pieces = []
    value_pieces = []
    for head in range(HEADS):
        lower = head * HEAD
        score_part = score_grads[head]
        prob_part = prob_list[head]
        key_pieces.append(rows_product(score_part, queries[:, lower : lower + HEAD]) * scale)
        value_pieces.append(rows_product(prob_part, d_mixed[:, lower : lower + HEAD]))
    key_value_grads = lax.psum_scatter(
        jnp.concatenate(key_pieces + value_pieces, axis=1).astype(jnp.bfloat16),
        "node",
        scatter_dimension=0,
        tiled=True,
    ).astype(jnp.float32)
    d_keys = key_value_grads[:, :width].astype(jnp.bfloat16)
    d_values = key_value_grads[:, width:].astype(jnp.bfloat16)
    normalized_gradient = (
        cols_product(d_queries, query_weight)
        + cols_product(d_keys, key_weight)
        + cols_product(d_values, value_weight)
    )
    node_state_gradient = (
        grads_in.astype(jnp.float32)
        + inverse_norm_scale
        * (
            normalized_gradient
            - centered_states
            * jnp.mean(normalized_gradient * centered_states, axis=1, keepdims=True)
        )
    ).astype(jnp.bfloat16)
    partial_query = rows_product(normalized_states, d_queries)
    partial_key = rows_product(normalized_states, d_keys)
    partial_value = rows_product(normalized_states, d_values)
    total_query, total_key, total_value, total_out = lax.psum(
        (partial_query, partial_key, partial_value, partial_out), ("node", "rep")
    )
    return (
        updated[None],
        node_state_gradient[None],
        total_query,
        total_key,
        total_value,
        total_out,
    )


def solution(mesh):
    in_specs = (
        P(("groups", "rep"), "node", None),
        P(("groups", "rep"), "node", None),
        P(("groups", "rep"), "node", None),
        P(("groups", "rep"), "node"),
        P(("groups", "rep"), None),
        P(),
        P(),
        P(),
        P(),
        P(),
    )
    out_specs = (
        P(("groups", "rep"), "node", None),
        P(("groups", "rep"), "node", None),
        P("groups", None),
        P("groups", None),
        P("groups", None),
        P("groups", None),
    )
    return jax.shard_map(
        on_device, mesh=mesh, in_specs=in_specs, out_specs=out_specs, check_vma=False
    )
```

profile of v0, /device:TPU:0, one launch (start us, length us, event | category | flops | bytes accessed | tf_op | source)
XLA Modules:
  0.0 189.7 jit_solution(12456625626089858018)
XLA Ops:
  7.3 0.6 copy-done.12
  8.0 0.7 copy-done.10
  8.9 0.6 copy-done.13
  9.5 1.0 fusion.42
  11.0 0.6 copy-done.11
  11.6 0.6 convolution_bitcast_fusion
  13.4 0.3 convolution_convert_fusion.3
  13.6 0.3 copy-done.5
  14.1 0.2 convolution_convert_fusion.1
  14.4 15.6 %all_gather.7 = bf16[512,256]{1,0:T(8,128)(2,1)S(1)} all-gather(bf16[128,256]{1,0:T(8,128)(2,1)S(1)} %convolution_convert_fusion.1), channel_id=1, replica_groups=mesh['groups'=2,'node'=4,'rep'=4] {'node'}, dimensions={0}, use_global_device_ids=true | all-gather | bytes 327680 | tf_op jit(solution)/shard_map/all_gather | solution.py:89
  30.0 14.6 %all_gather.6 = bf16[512,256]{1,0:T(8,128)(2,1)S(1)} all-gather(bf16[128,256]{1,0:T(8,128)(2,1)S(1)} %convolution_convert_fusion.2), channel_id=1, replica_groups=mesh['groups'=2,'node'=4,'rep'=4] {'node'}, dimensions={0}, use_global_device_ids=true | all-gather | bytes 327680 | tf_op jit(solution)/shard_map/all_gather | solution.py:88
  44.6 0.4 fusion.46
  45.0 0.4 fusion.43
  45.4 0.3 fusion.124
  45.7 0.4 fusion.127
  46.0 0.4 fusion.44
  46.4 0.3 fusion.126
  46.7 0.4 fusion.45
  47.1 0.4 fusion.125
  47.5 0.4 select_reduce_fusion.3
  47.9 0.3 select_convert_fusion.3
  48.2 0.3 convolution_convert_fusion.10
  48.7 0.3 convolution_convert_fusion.8
  49.0 0.4 copy-done.3
  49.9 0.2 multiply_reduce_fusion.3
  50.3 0.3 fusion.14
  50.8 0.3 fusion.16
  51.3 0.3 fusion.21
  51.8 0.3 fusion.25
  52.7 1.0 copy.27
  54.0 0.3 fusion.31
  54.3 0.3 fusion.33
  54.8 0.2 fusion.105
  55.0 1.0 fusion.50
  56.0 1.1 fusion.104
  57.1 19.4 %reduce-scatter.4.cloned.1.call-done = bf16[128,512]{1,0:T(8,128)(2,1)} async-done(((bf16[512,512]{1,0:T(8,128)(2,1)}), bf16[128,512]{1,0:T(8,128)(2,1)}) %reduce-scatter.4.cloned.1.call-update) | async-done | bytes 131088
  76.5 2.0 %fusion.78 = f32[512,256]{1,0:T(8,128)} fusion(bf16[128,512]{1,0:T(8,128)(2,1)} %reduce-scatter.4.cloned.1.call-done, bf16[1,128,512]{2,1,0:T(8,128)(2,1)S(1)} %copy-done.1, f32[128]{0:T(128)S(1)} %add_rsqrt_fusion), kind=kOutput, calls=%fused_computation.125 | convolution fusion | flops 33751040 | bytes 721408 | tf_op jit(solution)/shard_map/dot_general | solution.py:18
  78.5 1.1 fusion.75
  79.6 0.9 fusion.17
  80.7 0.3 fusion.37
  81.1 0.8 fusion.49
  81.9 95.8 %all-reduce.3.cloned.1.call-done = (f32[512,256]{1,0:T(8,128)}, f32[512,256]{1,0:T(8,128)}, f32[512,256]{1,0:T(8,128)}, f32[256,512]{1,0:T(8,128)}) async-done(((f32[512,256]{1,0:T(8,128)}, f32[512,256]{1,0:T(8,128)}, f32[512,256]{1,0:T(8,128)}, f32[256,512]{1,0:T(8,128)}), (f32[512,256]{1,0:T(8,128)}, f32[512,256]{1,0:T(8,128)}, f32[512,256]{1,0:T(8,128)}, ...) | async-done | bytes 2097168 | tf_op jit(solution)/shard_map/psum | solution.py:183
  177.7 1.9 %copy.53 = f32[512,256]{1,0:T(8,128)} copy(f32[512,256]{1,0:T(8,128)} %get-tuple-element.43) | data formatting | bytes 1048576
  179.6 0.8 copy.54
  180.4 0.4 copy-done.7
  180.8 0.8 copy.55
  181.6 0.4 copy-done.6
  182.0 0.8 copy.56
  (60 shorter events, 5.0 us)
Async XLA Ops:
  7.2 7.0 %copy-start = (bf16[512,256]{1,0:T(8,128)(2,1)S(1)}, bf16[512,256]{1,0:T(8,128)(2,1)}, u32[]{:S(2)}) copy-start(bf16[512,256]{1,0:T(8,128)(2,1)} %param.17) | copy-start | bytes 786436
  7.2 69.3 %reduce-scatter.4.cloned.1.call-start = ((), (), s32[]{:S(2)}) async-start(), calls=%async_computation.1 | async-start | bytes 655360
  7.3 0.7 copy-start.12
  8.0 0.7 copy-start.10
  8.8 0.7 copy-start.13
  10.9 0.7 copy-start.11
  11.6 1.7 copy-start.4
  12.3 1.0 copy-start.1
  12.9 1.0 copy-start.5
  48.5 1.0 copy-start.3
  48.7 0.9 copy-start.2
  53.7 123.9 %all-reduce.3.cloned.1.call-start = ((), (), s32[]{:S(2)}) async-start(), calls=%async_computation.2 | async-start | bytes 4194304 | tf_op jit(solution)/shard_map/psum | solution.py:183
  76.5 2.0 %copy-start.9 = (bf16[128,512]{1,0:T(8,128)(2,1)S(1)}, bf16[128,512]{1,0:T(8,128)(2,1)}, u32[]{:S(2)}) copy-start(bf16[128,512]{1,0:T(8,128)(2,1)} %reduce-scatter.4.cloned.1.call-done) | copy-start | bytes 393220
  177.6 1.9 %copy-start.8 = (f32[512,256]{1,0:T(8,128)S(1)}, f32[512,256]{1,0:T(8,128)}, u32[]{:S(2)}) copy-start(f32[512,256]{1,0:T(8,128)} %get-tuple-element.44) | copy-start | bytes 1572868
  179.6 1.2 copy-start.7
  180.8 1.2 copy-start.6
Sparse Core Ops, SparseCore 0:
  53.8 22.5 reduce-scatter.3
  81.0 96.5 all-reduce.2
where the time goes:
time: 190 us
  waiting for transfers between devices  115 us (61%)
  blocking collectives  30.2 us (16%)
  matrix products  16.7 us (9%)
  between operations  14.3 us (8%)
  local copies, waits for them, and re-layouts  10.3 us (5%)
  other arithmetic  2.95 us (2%)
    psum x1, waiting for transfers between devices, on_device(): lax.psum((partial_query, partial_key, partial_value, partial_out), ('node...  95.8 us
    unnamed x3, waiting for transfers between devices  19.4 us
    all_gather x1, blocking collectives, on_device(): lax.all_gather(values, 'node', axis=0, tiled=True)  15.6 us
    all_gather x1, blocking collectives, on_device(): lax.all_gather(keys, 'node', axis=0, tiled=True)  14.6 us
    unnamed x33, local copies, waits for them, and re-layouts  9.64 us
    dot_general x12, matrix products, rows_product(): lax.dot_general(left, right, CONTRACT_ROWS, preferred_element_type=jnp.fl...  6.81 us
  transfers between devices with their start and end apart: 2, of which 2 were waited for; matrix products, arithmetic and copies ran while one was open for 3% of the time, Pallas kernels for 0%

commit v1 on v0

--- a/solution.py
+++ b/solution.py
@@ -12,6 +12,22 @@
 HIGH = lax.Precision.HIGHEST
 CONTRACT_ROWS = (((0,), (0,)), ((), ()))
 CONTRACT_COLS = (((1,), (1,)), ((), ()))
+
+
+def gather_around(x, axis, dim):
+    ways, here, hop = (lax.axis_size(axis), lax.axis_index(axis), x.shape[dim])
+    shape = [n * ways if d == dim else n for d, n in enumerate(x.shape)]
+    full = lax.dynamic_update_slice_in_dim(jnp.zeros(shape, x.dtype), x, here * hop, axis=dim)
+    going_up = going_down = x
+    for far in range(1, ways // 2 + 1):
+        going_up = lax.ppermute(going_up, axis, [(d, (d + 1) % ways) for d in range(ways)])
+        full = lax.dynamic_update_slice_in_dim(full, going_up, (here - far) % ways * hop, axis=dim)
+        if 2 * far < ways:
+            going_down = lax.ppermute(going_down, axis, [(d, (d - 1) % ways) for d in range(ways)])
+            full = lax.dynamic_update_slice_in_dim(
+                full, going_down, (here + far) % ways * hop, axis=dim
+            )
+    return full
 
 
 def rows_product(left, right):
@@ -85,7 +101,7 @@
         jnp.bfloat16
     )
     keys_all, values_all = (
-        lax.all_gather(keys, "node", axis=0, tiled=True),
+        gather_around(keys, "node", 0),
         lax.all_gather(values, "node", axis=0, tiled=True),
     )
     levels, onehot, level_bias = level_tables(starts, total, bias_table)

time: 190 us -> 182 us (0.958)
  blocking collectives: 30.2 us -> 14.3 us
  starting transfers between devices: 0.08 us -> 5.27 us
  waiting for transfers between devices: 115 us -> 119 us
    all_gather x1 -> x0, blocking collectives: 14.6 us -> none  [on_device(): lax.all_gather(keys, 'node', axis=0, tiled=True)]
    ppermute x0 -> x3, waiting for transfers between devices: none -> 6.01 us  [the longest x2 6.01 us: gather_around(): lax.ppermute(going_up, axis, [(d, (d + 1) % ways) for d in range(ways)])]
    ppermute x0 -> x3, starting transfers between devices: none -> 5.19 us  [the longest x2 3.1 us: gather_around(): lax.ppermute(going_up, axis, [(d, (d + 1) % ways) for d in range(ways)])]
    unnamed x3, waiting for transfers between devices: 19.4 us -> 17.3 us
  transfers between devices with their start and end apart: 2 -> 5, of which waited for: 2 -> 3; matrix products, arithmetic and copies ran while one was open for 3% -> 5% of each run, Pallas kernels for 0% -> 0%
where the time goes in v1:
time: 182 us
  waiting for transfers between devices  119 us (65%)
  matrix products  16.7 us (9%)
  between operations  14.4 us (8%)
  blocking collectives  14.3 us (8%)
  local copies, waits for them, and re-layouts  8.85 us (5%)
  starting transfers between devices  5.27 us (3%)
  other arithmetic  2.99 us (2%)
    psum x1, waiting for transfers between devices, on_device(): lax.psum((partial_query, partial_key, partial_value, partial_out), ('node...  95.7 us
    unnamed x3, waiting for transfers between devices  17.3 us
    all_gather x1, blocking collectives, on_device(): lax.all_gather(values, 'node', axis=0, tiled=True)  14.3 us
    unnamed x33, local copies, waits for them, and re-layouts  8.18 us
    dot_general x12, matrix products, rows_product(): lax.dot_general(left, right, CONTRACT_ROWS, preferred_element_type=jnp.fl...  6.83 us
    ppermute x2, waiting for transfers between devices, gather_around(): lax.ppermute(going_up, axis, [(d, (d + 1) % ways) for d in range(ways)])  6.01 us
  transfers between devices with their start and end apart: 5, of which 3 were waited for; matrix products, arithmetic and copies ran while one was open for 5% of the time, Pallas kernels for 0%

profile of v1, /device:TPU:0, one launch (start us, length us, event | category | flops | bytes accessed | tf_op | source)
XLA Modules:
  0.0 181.6 jit_solution(5783134919929283896)
XLA Ops:
  7.2 1.0 fusion.42
  8.3 0.9 copy-done.1
  9.2 0.2 constant_dynamic-update-slice_fusion.3
  9.4 3.1 %collective-permute-start = (bf16[128,256]{1,0:T(8,128)(2,1)S(1)}, bf16[128,256]{1,0:T(8,128)(2,1)S(1)}, u32[]{:S(2)}, u32[]{:S(2)}) collective-permute-start(bf16[128,256]{1,0:T(8,128)(2,1)S(1)} %get-tuple-element.27), channel_id=1, source_target_pairs={{0,4},{4,8},{8,12},{12,0},{1,5},{5,9},{9,13},{13,1},{2,6},{6,10},{... | collective-permute-start | bytes 196616 | tf_op jit(solution)/shard_map/ppermute | solution.py:23
  12.5 2.1 %collective-permute-start.1 = (bf16[128,256]{1,0:T(8,128)(2,1)S(1)}, bf16[128,256]{1,0:T(8,128)(2,1)S(1)}, u32[]{:S(2)}, u32[]{:S(2)}) collective-permute-start(bf16[128,256]{1,0:T(8,128)(2,1)S(1)} %get-tuple-element.27), channel_id=1, source_target_pairs={{0,12},{4,0},{8,4},{12,8},{1,13},{5,1},{9,5},{13,9},{2,14},{6,2},{... | collective-permute-start | bytes 196616 | tf_op jit(solution)/shard_map/ppermute | solution.py:26
  14.7 0.6 copy-done.12
  16.1 0.6 convolution_bitcast_fusion
  17.0 0.2 convolution_convert_fusion.3
  17.4 0.2 fusion.90
  18.1 0.3 convolution_convert_fusion.1
  18.4 0.4 fusion.46
  18.8 0.4 fusion.43
  19.2 0.4 fusion.44
  19.6 0.4 fusion.45
  20.1 0.4 copy-done.2
  20.7 14.3 %all_gather.3 = bf16[512,256]{1,0:T(8,128)(2,1)S(1)} all-gather(bf16[128,256]{1,0:T(8,128)(2,1)S(1)} %convolution_convert_fusion.1), channel_id=1, replica_groups=mesh['groups'=2,'node'=4,'rep'=4] {'node'}, dimensions={0}, use_global_device_ids=true | all-gather | bytes 327680 | tf_op jit(solution)/shard_map/all_gather | solution.py:105
  35.1 6.0 %collective-permute-done.2 = bf16[128,256]{1,0:T(8,128)(2,1)S(1)} collective-permute-done((bf16[128,256]{1,0:T(8,128)(2,1)S(1)}, bf16[128,256]{1,0:T(8,128)(2,1)S(1)}, u32[]{:S(2)}, u32[]{:S(2)}) %collective-permute-start.2) | collective-permute-done | bytes 65568 | tf_op jit(solution)/shard_map/ppermute | solution.py:23
  41.1 0.4 fusion.127
  41.5 0.3 fusion.126
  41.7 0.4 fusion.125
  42.1 0.3 fusion.124
  42.4 0.4 select_reduce_fusion.3
  42.8 0.3 select_convert_fusion.3
  43.1 0.3 convolution_convert_fusion.10
  43.6 0.3 convolution_convert_fusion.8
  44.8 0.3 fusion.14
  45.1 0.3 fusion.31
  45.6 0.3 fusion.16
  45.8 0.3 fusion.21
  46.3 0.3 fusion.25
  47.2 1.0 copy.27
  48.3 0.3 fusion.33
  48.8 0.2 fusion.105
  49.0 1.0 fusion.50
  50.0 1.1 fusion.104
  51.2 17.3 %reduce-scatter.4.cloned.1.call-done = bf16[128,512]{1,0:T(8,128)(2,1)} async-done(((bf16[512,512]{1,0:T(8,128)(2,1)}), bf16[128,512]{1,0:T(8,128)(2,1)}) %reduce-scatter.4.cloned.1.call-update) | async-done | bytes 131088
  68.5 2.0 %fusion.78 = f32[512,256]{1,0:T(8,128)} fusion(bf16[128,512]{1,0:T(8,128)(2,1)} %reduce-scatter.4.cloned.1.call-done, bf16[1,128,512]{2,1,0:T(8,128)(2,1)S(1)} %copy-done.1, f32[128]{0:T(128)S(1)} %add_rsqrt_fusion), kind=kOutput, calls=%fused_computation.125 | convolution fusion | flops 33751040 | bytes 721408 | tf_op jit(solution)/shard_map/dot_general | solution.py:34
  70.5 1.1 fusion.75
  71.6 0.9 fusion.17
  72.7 0.3 fusion.37
  73.1 0.8 fusion.49
  73.9 95.7 %all-reduce.3.cloned.1.call-done = (f32[512,256]{1,0:T(8,128)}, f32[512,256]{1,0:T(8,128)}, f32[512,256]{1,0:T(8,128)}, f32[256,512]{1,0:T(8,128)}) async-done(((f32[512,256]{1,0:T(8,128)}, f32[512,256]{1,0:T(8,128)}, f32[512,256]{1,0:T(8,128)}, f32[256,512]{1,0:T(8,128)}), (f32[512,256]{1,0:T(8,128)}, f32[512,256]{1,0:T(8,128)}, f32[512,256]{1,0:T(8,128)}, ...) | async-done | bytes 2097168 | tf_op jit(solution)/shard_map/psum | solution.py:199
  169.5 1.9 %copy.57 = f32[512,256]{1,0:T(8,128)} copy(f32[512,256]{1,0:T(8,128)} %get-tuple-element.45) | data formatting | bytes 1048576
  171.5 0.8 copy.58
  172.3 0.4 copy-done.7
  172.7 0.8 copy.59
  173.5 0.4 copy-done.6
  173.9 0.8 copy.60
  (69 shorter events, 4.8 us)
Async XLA Ops:
  7.2 1.2 copy-start
  7.2 61.3 %reduce-scatter.4.cloned.1.call-start = ((), (), s32[]{:S(2)}) async-start(), calls=%async_computation.1 | async-start | bytes 655360
  8.3 0.9 copy-start.1
  9.4 25.6 %collective-permute-start = (bf16[128,256]{1,0:T(8,128)(2,1)S(1)}, bf16[128,256]{1,0:T(8,128)(2,1)S(1)}, u32[]{:S(2)}, u32[]{:S(2)}) collective-permute-start(bf16[128,256]{1,0:T(8,128)(2,1)S(1)} %get-tuple-element.27), channel_id=1, source_target_pairs={{0,4},{4,8},{8,12},{12,0},{1,5},{5,9},{9,13},{13,1},{2,6},{6,10},{... | collective-permute-start | bytes 196616 | tf_op jit(solution)/shard_map/ppermute | solution.py:23
  12.5 22.5 %collective-permute-start.1 = (bf16[128,256]{1,0:T(8,128)(2,1)S(1)}, bf16[128,256]{1,0:T(8,128)(2,1)S(1)}, u32[]{:S(2)}, u32[]{:S(2)}) collective-permute-start(bf16[128,256]{1,0:T(8,128)(2,1)S(1)} %get-tuple-element.27), channel_id=1, source_target_pairs={{0,12},{4,0},{8,4},{12,8},{1,13},{5,1},{9,5},{13,9},{2,14},{6,2},{... | collective-permute-start | bytes 196616 | tf_op jit(solution)/shard_map/ppermute | solution.py:26
  14.6 0.7 copy-start.12
  14.6 1.0 copy-start.13
  14.6 1.1 copy-start.10
  14.6 1.5 copy-start.11
  14.6 2.3 %copy-start.5 = (bf16[512,256]{1,0:T(8,128)(2,1)S(1)}, bf16[512,256]{1,0:T(8,128)(2,1)}, u32[]{:S(2)}) copy-start(bf16[512,256]{1,0:T(8,128)(2,1)} %param.15) | copy-start | bytes 786436
  17.0 1.1 copy-start.3
  19.2 1.0 copy-start.4
  19.6 0.9 copy-start.2
  35.0 6.1 %collective-permute-start.2 = (bf16[128,256]{1,0:T(8,128)(2,1)S(1)}, bf16[128,256]{1,0:T(8,128)(2,1)S(1)}, u32[]{:S(2)}, u32[]{:S(2)}) collective-permute-start(bf16[128,256]{1,0:T(8,128)(2,1)S(1)} %collective-permute-done), channel_id=1, source_target_pairs={{0,4},{4,8},{8,12},{12,0},{1,5},{5,9},{9,13},{13,1},{2,6},{6,10},{... | collective-permute-start | bytes 196616 | tf_op jit(solution)/shard_map/ppermute | solution.py:23
  48.3 121.3 %all-reduce.3.cloned.1.call-start = ((), (), s32[]{:S(2)}) async-start(), calls=%async_computation.2 | async-start | bytes 4194304 | tf_op jit(solution)/shard_map/psum | solution.py:199
  68.5 2.0 %copy-start.9 = (bf16[128,512]{1,0:T(8,128)(2,1)S(1)}, bf16[128,512]{1,0:T(8,128)(2,1)}, u32[]{:S(2)}) copy-start(bf16[128,512]{1,0:T(8,128)(2,1)} %reduce-scatter.4.cloned.1.call-done) | copy-start | bytes 393220
  169.5 1.9 %copy-start.8 = (f32[512,256]{1,0:T(8,128)S(1)}, f32[512,256]{1,0:T(8,128)}, u32[]{:S(2)}) copy-start(f32[512,256]{1,0:T(8,128)} %get-tuple-element.46) | copy-start | bytes 1572868
  171.5 1.2 copy-start.7
  172.7 1.2 copy-start.6
Sparse Core Ops, SparseCore 0:
  48.4 20.0 reduce-scatter.3
  73.0 96.4 all-reduce.2
